TPU v7x, 256 devices: a whole 4x4x8 slice. The times are simulated.
256 devices in a mesh: peer: 8 (over x, y_hi), space: 32 (over y_lo, z, core).
Axes of the slice: x: 4, y: 4 (y_hi: 2, y_lo: 2; y = y_hi * 2 + y_lo), z: 8, core: 2. Of those that a mesh axis runs over, the one named last changes fastest.
Arguments:
- images: bfloat16 [8, 512, 32, 512], P('peer', 'space'), may hold values from -6 to 6
- task_grad: bfloat16 [8, 512, 32, 512], P('peer', 'space'), may hold values from -6 to 6
- pairing: int32 [8], replicated, may hold values from 0 to 7, as said below
- first_kernel: bfloat16 [8, 3, 3, 512, 512], P('peer'), may hold values from -0.09375 to 0.09375
- first_scale: float32 [8, 512], P('peer'), may hold values from 0.25 to 1.75
- first_shift: float32 [8, 512], P('peer'), may hold values from -3 to 3
- second_kernel: bfloat16 [8, 3, 3, 512, 512], P('peer'), may hold values from -0.09375 to 0.09375
- second_scale: float32 [8, 512], P('peer'), may hold values from 0.25 to 1.75
- second_shift: float32 [8, 512], P('peer'), may hold values from -3 to 3
Outputs:
- input_grad: bfloat16 [8, 512, 32, 512], P('peer', 'space')
Inputs may be any that keep to these rules, and one draw needn't show every extreme that they name: `pairing`: every network index appears exactly once.
All inputs are finite; a program needn't handle non-finite values.
Results may differ from a plain program's by a relative error of at most 0.012.
Values may be sent and summed in bfloat16 or wider, within the bound.
A program may use at most 64 MiB of HBM per device.

v0:
```python
import jax
import jax.numpy as jnp
from jax import lax
from jax.sharding import PartitionSpec as P


def extended(cells, sides, width):
    for axis, dim in sides:
        count = lax.axis_size(axis)
        ends = count - 1
        head = lax.slice_in_dim(cells, 0, width, axis=dim)
        tail = lax.slice_in_dim(cells, cells.shape[dim] - width, cells.shape[dim], axis=dim)
        cells = jnp.concatenate(
            [
                lax.ppermute(tail, axis, [(i, (i + 1) % count) for i in range(ends)]),
                cells,
                lax.ppermute(head, axis, [((i + 1) % count, i) for i in range(ends)]),
            ],
            axis=dim,
        )
    return cells


def apply_dilated_filter(
    padded_row_count, filter_kernel, dilation_rate, output_rows, reverse_kernel
):
    input_width = padded_row_count.shape[1]
    padded_input = jnp.pad(padded_row_count, ((0, 0), (dilation_rate, dilation_rate), (0, 0)))
    total = jnp.zeros((output_rows, input_width, filter_kernel.shape[2]), jnp.float32)
    for kernel_tap_row in range(3):
        for kernel_tap_column in range(3):
            input_window = padded_input[
                kernel_tap_row * dilation_rate : kernel_tap_row * dilation_rate + output_rows,
                kernel_tap_column * dilation_rate : kernel_tap_column * dilation_rate + input_width,
            ]
            if reverse_kernel:
                total = total + jnp.einsum(
                    "rwo,io->rwi",
                    input_window,
                    filter_kernel[2 - kernel_tap_row, 2 - kernel_tap_column],
                    preferred_element_type=jnp.float32,
                )
            else:
                total = total + jnp.einsum(
                    "rwi,io->rwo",
                    input_window,
                    filter_kernel[kernel_tap_row, kernel_tap_column],
                    preferred_element_type=jnp.float32,
                )
    return total


def silu_slope(value):
    sig = jax.nn.sigmoid(value)
    return sig * (1.0 + value * (1.0 - sig))


def per_device(
    images,
    task_grad,
    pairing,
    first_kernel,
    first_scale,
    first_shift,
    second_kernel,
    second_scale,
    second_shift,
):
    image = images[0]
    strip_rows = image.shape[0]
    kernel_one = first_kernel[0]
    kernel_two = second_kernel[0]
    scale_one = first_scale[0]
    shift_one = first_shift[0]
    scale_two = second_scale[0]
    shift_two = second_shift[0]
    image_ext = extended(image, (("space", 0),), 2)
    pre_first = (
        scale_one * apply_dilated_filter(image_ext, kernel_one, 2, strip_rows, False) + shift_one
    )
    hidden = jax.nn.silu(pre_first).astype(jnp.bfloat16)
    hidden_ext = extended(hidden, (("space", 0),), 4)
    pre_second = (
        scale_two * apply_dilated_filter(hidden_ext, kernel_two, 4, strip_rows, False) + shift_two
    )
    feat = jax.nn.silu(pre_second).astype(jnp.bfloat16)
    partner = pairing[lax.axis_index("peer")]
    piece = lax.all_gather(feat[None], "peer", axis=0, tiled=True)
    owners = jnp.arange(piece.shape[0], dtype=jnp.int32)
    pick = (owners == partner).astype(jnp.bfloat16)
    partner_feat = jnp.einsum("k,krwc->rwc", pick, piece, preferred_element_type=jnp.float32)
    cot = task_grad[0].astype(jnp.float32) + feat.astype(jnp.float32) - partner_feat
    grad_second = (cot * silu_slope(pre_second) * scale_two).astype(jnp.bfloat16)
    grad_second_ext = extended(grad_second, (("space", 0),), 4)
    grad_hidden = apply_dilated_filter(grad_second_ext, kernel_two, 4, strip_rows, True)
    grad_first = (grad_hidden * silu_slope(pre_first) * scale_one).astype(jnp.bfloat16)
    grad_first_ext = extended(grad_first, (("space", 0),), 2)
    input_grad = apply_dilated_filter(grad_first_ext, kernel_one, 2, strip_rows, True).astype(
        jnp.bfloat16
    )
    return input_grad[None]


def solution(mesh):
    placed = (
        P("peer", "space", None, None),
        P("peer", "space", None, None),
        P(),
        P("peer", None, None, None, None),
        P("peer", None),
        P("peer", None),
        P("peer", None, None, None, None),
        P("peer", None),
        P("peer", None),
    )
    return jax.shard_map(
        per_device,
        mesh=mesh,
        in_specs=placed,
        out_specs=P("peer", "space", None, None),
        check_vma=False,
    )
```

profile of v0, /device:TPU:97, one launch (start us, length us, event | category | flops | bytes accessed | tf_op | source)
XLA Modules:
  0.0 163.8 jit_solution(12028353491544414029)
XLA Ops:
  6.5 1.0 slice_bitcast_fusion.55
  7.6 5.4 %collective-permute-start = (bf16[2,32,512]{2,1,0:T(8,128)(2,1)S(1)}, bf16[2,32,512]{2,1,0:T(8,128)(2,1)S(1)}, u32[]{:S(2)}, u32[]{:S(2)}) collective-permute-start(bf16[2,32,512]{2,1,0:T(8,128)(2,1)S(1)} %get-tuple-element.11), channel_id=1, source_target_pairs={{0,1},{1,2},{2,3},{3,4},{4,5},{5,6},{6,7},{7,8},{8,9},{9,10},{10,1... | collective-permute-start | bytes 196616 | tf_op jit(solution)/shard_map/ppermute | solution.py:15
  13.0 1.9 %collective-permute-start.1 = (bf16[2,32,512]{2,1,0:T(8,128)(2,1)S(1)}, bf16[2,32,512]{2,1,0:T(8,128)(2,1)S(1)}, u32[]{:S(2)}, u32[]{:S(2)}) collective-permute-start(bf16[2,32,512]{2,1,0:T(8,128)(2,1)S(1)} %get-tuple-element.12), channel_id=1, source_target_pairs={{1,0},{2,1},{3,2},{4,3},{5,4},{6,5},{7,6},{8,7},{9,8},{10,9},{11,1... | collective-permute-start | bytes 196616 | tf_op jit(solution)/shard_map/ppermute | solution.py:17
  15.0 4.9 %collective-permute-done.1 = bf16[2,32,512]{2,1,0:T(8,128)(2,1)S(1)} collective-permute-done((bf16[2,32,512]{2,1,0:T(8,128)(2,1)S(1)}, bf16[2,32,512]{2,1,0:T(8,128)(2,1)S(1)}, u32[]{:S(2)}, u32[]{:S(2)}) %collective-permute-start.1) | collective-permute-done | bytes 65568 | tf_op jit(solution)/shard_map/ppermute | solution.py:17
  19.8 1.4 fusion.30
  21.2 1.5 fusion.80
  22.7 1.6 fusion.45
  27.1 0.7 multiply_convert_fusion.1
  27.8 2.1 %collective-permute-start.2 = (bf16[4,32,512]{2,1,0:T(8,128)(2,1)S(1)}, bf16[4,32,512]{2,1,0:T(8,128)(2,1)S(1)}, u32[]{:S(2)}, u32[]{:S(2)}) collective-permute-start(bf16[4,32,512]{2,1,0:T(8,128)(2,1)S(1)} %get-tuple-element.9), channel_id=1, source_target_pairs={{0,1},{1,2},{2,3},{3,4},{4,5},{5,6},{6,7},{7,8},{8,9},{9,10},{10,1... | collective-permute-start | bytes 393224 | tf_op jit(solution)/shard_map/ppermute | solution.py:15
  29.9 2.4 %collective-permute-start.3 = (bf16[4,32,512]{2,1,0:T(8,128)(2,1)S(1)}, bf16[4,32,512]{2,1,0:T(8,128)(2,1)S(1)}, u32[]{:S(2)}, u32[]{:S(2)}) collective-permute-start(bf16[4,32,512]{2,1,0:T(8,128)(2,1)S(1)} %get-tuple-element.10), channel_id=1, source_target_pairs={{1,0},{2,1},{3,2},{4,3},{5,4},{6,5},{7,6},{8,7},{9,8},{10,9},{11,1... | collective-permute-start | bytes 393224 | tf_op jit(solution)/shard_map/ppermute | solution.py:17
  32.3 5.1 %collective-permute-done.3 = bf16[4,32,512]{2,1,0:T(8,128)(2,1)S(1)} collective-permute-done((bf16[4,32,512]{2,1,0:T(8,128)(2,1)S(1)}, bf16[4,32,512]{2,1,0:T(8,128)(2,1)S(1)}, u32[]{:S(2)}, u32[]{:S(2)}) %collective-permute-start.3) | collective-permute-done | bytes 131104 | tf_op jit(solution)/shard_map/ppermute | solution.py:17
  41.4 1.5 multiply_convert_fusion
  43.0 0.6 dynamic_slice.3
  43.5 74.3 %all-gather.3.cloned.1.call-done = bf16[128,32,512]{2,1,0:T(8,128)(2,1)} async-done(((bf16[16,32,512]{2,1,0:T(8,128)(2,1)}), bf16[128,32,512]{2,1,0:T(8,128)(2,1)}) %all-gather.3.cloned.1.call-update) | async-done | bytes 4194320 | tf_op jit(solution)/shard_map/all_gather | solution.py:88
  117.9 5.9 %fusion = f32[1,16,32,512]{3,0,2,1:T(1,128)S(1)} fusion(bf16[8,16,32,512]{3,2,1,0:T(8,128)(2,1)} %bitcast.184, s32[]{:T(128)} %bitcast.46), kind=kOutput, calls=%fused_computation | convolution fusion | flops 4194312 | bytes 5242884 | tf_op jit(solution)/shard_map/k,krwc->rwc/dot_general | solution.py:91
  123.8 0.6 fusion.20
  124.4 5.7 %collective-permute-start.4 = (bf16[4,32,512]{2,1,0:T(8,128)(2,1)S(1)}, bf16[4,32,512]{2,1,0:T(8,128)(2,1)S(1)}, u32[]{:S(2)}, u32[]{:S(2)}) collective-permute-start(bf16[4,32,512]{2,1,0:T(8,128)(2,1)S(1)} %get-tuple-element.7), channel_id=1, source_target_pairs={{0,1},{1,2},{2,3},{3,4},{4,5},{5,6},{6,7},{7,8},{8,9},{9,10},{10,1... | collective-permute-start | bytes 393224 | tf_op jit(solution)/shard_map/ppermute | solution.py:15
  130.0 2.1 %collective-permute-start.5 = (bf16[4,32,512]{2,1,0:T(8,128)(2,1)S(1)}, bf16[4,32,512]{2,1,0:T(8,128)(2,1)S(1)}, u32[]{:S(2)}, u32[]{:S(2)}) collective-permute-start(bf16[4,32,512]{2,1,0:T(8,128)(2,1)S(1)} %get-tuple-element.8), channel_id=1, source_target_pairs={{1,0},{2,1},{3,2},{4,3},{5,4},{6,5},{7,6},{8,7},{9,8},{10,9},{11,1... | collective-permute-start | bytes 393224 | tf_op jit(solution)/shard_map/ppermute | solution.py:17
  132.2 5.4 %collective-permute-done.5 = bf16[4,32,512]{2,1,0:T(8,128)(2,1)S(1)} collective-permute-done((bf16[4,32,512]{2,1,0:T(8,128)(2,1)S(1)}, bf16[4,32,512]{2,1,0:T(8,128)(2,1)S(1)}, u32[]{:S(2)}, u32[]{:S(2)}) %collective-permute-start.5) | collective-permute-done | bytes 131104 | tf_op jit(solution)/shard_map/ppermute | solution.py:17
  141.9 0.7 fusion.15
  142.6 2.1 %collective-permute-start.6 = (bf16[2,32,512]{2,1,0:T(8,128)(2,1)S(1)}, bf16[2,32,512]{2,1,0:T(8,128)(2,1)S(1)}, u32[]{:S(2)}, u32[]{:S(2)}) collective-permute-start(bf16[2,32,512]{2,1,0:T(8,128)(2,1)S(1)} %get-tuple-element.5), channel_id=1, source_target_pairs={{0,1},{1,2},{2,3},{3,4},{4,5},{5,6},{6,7},{7,8},{8,9},{9,10},{10,1... | collective-permute-start | bytes 196616 | tf_op jit(solution)/shard_map/ppermute | solution.py:15
  144.7 2.4 %collective-permute-start.7 = (bf16[2,32,512]{2,1,0:T(8,128)(2,1)S(1)}, bf16[2,32,512]{2,1,0:T(8,128)(2,1)S(1)}, u32[]{:S(2)}, u32[]{:S(2)}) collective-permute-start(bf16[2,32,512]{2,1,0:T(8,128)(2,1)S(1)} %get-tuple-element.6), channel_id=1, source_target_pairs={{1,0},{2,1},{3,2},{4,3},{5,4},{6,5},{7,6},{8,7},{9,8},{10,9},{11,1... | collective-permute-start | bytes 196616 | tf_op jit(solution)/shard_map/ppermute | solution.py:17
  147.1 4.4 %collective-permute-done.7 = bf16[2,32,512]{2,1,0:T(8,128)(2,1)S(1)} collective-permute-done((bf16[2,32,512]{2,1,0:T(8,128)(2,1)S(1)}, bf16[2,32,512]{2,1,0:T(8,128)(2,1)S(1)}, u32[]{:S(2)}, u32[]{:S(2)}) %collective-permute-start.7) | collective-permute-done | bytes 65568 | tf_op jit(solution)/shard_map/ppermute | solution.py:17
  155.7 1.3 fusion.16
  (73 shorter events, 15.1 us)
Async XLA Ops:
  6.5 111.3 %all-gather.3.cloned.1.call-start = ((), (), s32[]{:S(2)}) async-start(), calls=%async_computation | async-start | bytes 4718592 | tf_op jit(solution)/shard_map/all_gather | solution.py:88
  6.5 17.8 %copy-start = (bf16[1,3,3,512,512]{4,3,2,1,0:T(8,128)(2,1)S(1)}, bf16[1,3,3,512,512]{4,3,2,1,0:T(8,128)(2,1)}, u32[]{:S(2)}) copy-start(bf16[1,3,3,512,512]{4,3,2,1,0:T(8,128)(2,1)} %param.12) | copy-start | bytes 14155780
  7.6 7.4 %collective-permute-start = (bf16[2,32,512]{2,1,0:T(8,128)(2,1)S(1)}, bf16[2,32,512]{2,1,0:T(8,128)(2,1)S(1)}, u32[]{:S(2)}, u32[]{:S(2)}) collective-permute-start(bf16[2,32,512]{2,1,0:T(8,128)(2,1)S(1)} %get-tuple-element.11), channel_id=1, source_target_pairs={{0,1},{1,2},{2,3},{3,4},{4,5},{5,6},{6,7},{7,8},{8,9},{9,10},{10,1... | collective-permute-start | bytes 196616 | tf_op jit(solution)/shard_map/ppermute | solution.py:15
  13.0 6.8 %collective-permute-start.1 = (bf16[2,32,512]{2,1,0:T(8,128)(2,1)S(1)}, bf16[2,32,512]{2,1,0:T(8,128)(2,1)S(1)}, u32[]{:S(2)}, u32[]{:S(2)}) collective-permute-start(bf16[2,32,512]{2,1,0:T(8,128)(2,1)S(1)} %get-tuple-element.12), channel_id=1, source_target_pairs={{1,0},{2,1},{3,2},{4,3},{5,4},{6,5},{7,6},{8,7},{9,8},{10,9},{11,1... | collective-permute-start | bytes 196616 | tf_op jit(solution)/shard_map/ppermute | solution.py:17
  24.3 1.4 copy-start.1
  25.7 1.4 copy-start.4
  25.7 1.4 copy-start.6
  26.6 11.2 %slice-start = ((s8[4718592]{0:T(1024)(128)(4,1)}), s8[4194304]{0:T(1024)(128)(4,1)S(1)}, s32[]{:S(2)}) async-start(s8[4718592]{0:T(1024)(128)(4,1)} %bitcast.142), calls=%async_computation.1 | async-start | bytes 8388608
  27.1 10.7 %slice-start.1 = ((s8[4718592]{0:T(1024)(128)(4,1)}), s8[524288]{0:T(1024)(128)(4,1)S(1)}, s32[]{:S(2)}) async-start(s8[4718592]{0:T(1024)(128)(4,1)} %bitcast.142), calls=%async_computation.2 | async-start | bytes 1048576
  27.8 4.5 %collective-permute-start.2 = (bf16[4,32,512]{2,1,0:T(8,128)(2,1)S(1)}, bf16[4,32,512]{2,1,0:T(8,128)(2,1)S(1)}, u32[]{:S(2)}, u32[]{:S(2)}) collective-permute-start(bf16[4,32,512]{2,1,0:T(8,128)(2,1)S(1)} %get-tuple-element.9), channel_id=1, source_target_pairs={{0,1},{1,2},{2,3},{3,4},{4,5},{5,6},{6,7},{7,8},{8,9},{9,10},{10,1... | collective-permute-start | bytes 393224 | tf_op jit(solution)/shard_map/ppermute | solution.py:15
  29.9 7.5 %collective-permute-start.3 = (bf16[4,32,512]{2,1,0:T(8,128)(2,1)S(1)}, bf16[4,32,512]{2,1,0:T(8,128)(2,1)S(1)}, u32[]{:S(2)}, u32[]{:S(2)}) collective-permute-start(bf16[4,32,512]{2,1,0:T(8,128)(2,1)S(1)} %get-tuple-element.10), channel_id=1, source_target_pairs={{1,0},{2,1},{3,2},{4,3},{5,4},{6,5},{7,6},{8,7},{9,8},{10,9},{11,1... | collective-permute-start | bytes 393224 | tf_op jit(solution)/shard_map/ppermute | solution.py:17
  40.0 1.4 copy-start.3
  40.1 1.4 copy-start.5
  41.4 1.5 copy-start.7
  41.4 96.6 %slice-start.2 = ((s8[4718592]{0:T(1024)(128)(4,1)}), s8[524288]{0:T(1024)(128)(4,1)S(1)}, s32[]{:S(2)}) async-start(s8[4718592]{0:T(1024)(128)(4,1)} %bitcast.153), calls=%async_computation.3 | async-start | bytes 1048576
  42.9 80.8 %copy-start.2 = (bf16[1,16,32,512]{3,2,1,0:T(8,128)(2,1)S(1)}, bf16[1,16,32,512]{3,2,1,0:T(8,128)(2,1)}, u32[]{:S(2)}) copy-start(bf16[1,16,32,512]{3,2,1,0:T(8,128)(2,1)} %param.10) | copy-start | bytes 1572868
  117.9 20.2 %slice-start.3 = ((s8[4718592]{0:T(1024)(128)(4,1)}), s8[4194304]{0:T(1024)(128)(4,1)S(1)}, s32[]{:S(2)}) async-start(s8[4718592]{0:T(1024)(128)(4,1)} %bitcast.153), calls=%async_computation.4 | async-start | bytes 8388608
  124.4 7.8 %collective-permute-start.4 = (bf16[4,32,512]{2,1,0:T(8,128)(2,1)S(1)}, bf16[4,32,512]{2,1,0:T(8,128)(2,1)S(1)}, u32[]{:S(2)}, u32[]{:S(2)}) collective-permute-start(bf16[4,32,512]{2,1,0:T(8,128)(2,1)S(1)} %get-tuple-element.7), channel_id=1, source_target_pairs={{0,1},{1,2},{2,3},{3,4},{4,5},{5,6},{6,7},{7,8},{8,9},{9,10},{10,1... | collective-permute-start | bytes 393224 | tf_op jit(solution)/shard_map/ppermute | solution.py:15
  130.0 7.5 %collective-permute-start.5 = (bf16[4,32,512]{2,1,0:T(8,128)(2,1)S(1)}, bf16[4,32,512]{2,1,0:T(8,128)(2,1)S(1)}, u32[]{:S(2)}, u32[]{:S(2)}) collective-permute-start(bf16[4,32,512]{2,1,0:T(8,128)(2,1)S(1)} %get-tuple-element.8), channel_id=1, source_target_pairs={{1,0},{2,1},{3,2},{4,3},{5,4},{6,5},{7,6},{8,7},{9,8},{10,9},{11,1... | collective-permute-start | bytes 393224 | tf_op jit(solution)/shard_map/ppermute | solution.py:17
  141.4 10.5 %slice-start.4 = ((s8[4718592]{0:T(1024)(128)(4,1)}), s8[524288]{0:T(1024)(128)(4,1)S(1)}, s32[]{:S(2)}) async-start(s8[4718592]{0:T(1024)(128)(4,1)} %bitcast.173), calls=%async_computation.5 | async-start | bytes 1048576
  141.9 10.0 %slice-start.5 = ((s8[4718592]{0:T(1024)(128)(4,1)}), s8[4194304]{0:T(1024)(128)(4,1)S(1)}, s32[]{:S(2)}) async-start(s8[4718592]{0:T(1024)(128)(4,1)} %bitcast.173), calls=%async_computation.6 | async-start | bytes 8388608
  142.6 4.5 %collective-permute-start.6 = (bf16[2,32,512]{2,1,0:T(8,128)(2,1)S(1)}, bf16[2,32,512]{2,1,0:T(8,128)(2,1)S(1)}, u32[]{:S(2)}, u32[]{:S(2)}) collective-permute-start(bf16[2,32,512]{2,1,0:T(8,128)(2,1)S(1)} %get-tuple-element.5), channel_id=1, source_target_pairs={{0,1},{1,2},{2,3},{3,4},{4,5},{5,6},{6,7},{7,8},{8,9},{9,10},{10,1... | collective-permute-start | bytes 196616 | tf_op jit(solution)/shard_map/ppermute | solution.py:15
  144.7 6.8 %collective-permute-start.7 = (bf16[2,32,512]{2,1,0:T(8,128)(2,1)S(1)}, bf16[2,32,512]{2,1,0:T(8,128)(2,1)S(1)}, u32[]{:S(2)}, u32[]{:S(2)}) collective-permute-start(bf16[2,32,512]{2,1,0:T(8,128)(2,1)S(1)} %get-tuple-element.6), channel_id=1, source_target_pairs={{1,0},{2,1},{3,2},{4,3},{5,4},{6,5},{7,6},{8,7},{9,8},{10,9},{11,1... | collective-permute-start | bytes 196616 | tf_op jit(solution)/shard_map/ppermute | solution.py:17
Sparse Core Ops, SparseCore 0:
  43.1 74.7 all-gather.2
where the time goes:
time: 164 us
  waiting for transfers between devices  94 us (57%)
  matrix products  26.8 us (16%)
  starting transfers between devices  24.1 us (15%)
  between operations  14 us (9%)
  other arithmetic  3.18 us (2%)
  local copies, waits for them, and re-layouts  1.76 us (1%)
    all_gather x1, waiting for transfers between devices, per_device(): piece = lax.all_gather(feat[None], 'peer', axis=0, tiled=True)  74.3 us
    ppermute x4, waiting for transfers between devices, extended(): lax.ppermute(head, axis, [((i + 1) % count, i) for i in range(ends)])  19.7 us
    ppermute x4, starting transfers between devices, extended(): lax.ppermute(tail, axis, [(i, (i + 1) % count) for i in range(ends)])  15.2 us
    dot_general x18, matrix products, apply_dilated_filter(): jnp.einsum('rwi,io->rwo', input_window, filter_kernel[kernel_tap_row, ker...  11.4 us
    dot_general x18, matrix products, apply_dilated_filter(): jnp.einsum('rwo,io->rwi', input_window, filter_kernel[2 - kernel_tap_row,...  9.54 us
    ppermute x4, starting transfers between devices, extended(): lax.ppermute(head, axis, [((i + 1) % count, i) for i in range(ends)])  8.83 us
    dot_general x1, matrix products, per_device(): jnp.einsum('k,krwc->rwc', pick, piece, preferred_element_type=jnp.float32)  5.87 us
  transfers between devices with their start and end apart: 9, of which 5 were waited for; matrix products, arithmetic and copies ran while one was open for 0% of the time, Pallas kernels for 0%

commit v1 on v0

--- a/solution.py
+++ b/solution.py
@@ -85,7 +85,9 @@
     )
     feat = jax.nn.silu(pre_second).astype(jnp.bfloat16)
     partner = pairing[lax.axis_index("peer")]
-    piece = lax.all_gather(feat[None], "peer", axis=0, tiled=True)
+    piece = jnp.concatenate(
+        lax.all_to_all(jnp.stack([feat[None]] * lax.axis_size("peer")), "peer", 0, 0), axis=0
+    )
     owners = jnp.arange(piece.shape[0], dtype=jnp.int32)
     pick = (owners == partner).astype(jnp.bfloat16)
     partner_feat = jnp.einsum("k,krwc->rwc", pick, piece, preferred_element_type=jnp.float32)

time: 164 us -> 139 us (0.85)
  waiting for transfers between devices: 94 us -> 76.8 us
  between operations: 14 us -> 0.59 us
  starting transfers between devices: 24.1 us -> 28.1 us
  local copies, waits for them, and re-layouts: 1.76 us -> 4.29 us
    all_gather x1 -> x0, waiting for transfers between devices: 74.3 us -> none  [per_device(): piece = lax.all_gather(feat[None], 'peer', axis=0, tiled=True)]
    all_to_all x0 -> x1, waiting for transfers between devices: none -> 57.2 us  [per_device(): lax.all_to_all(jnp.stack([feat[None]] * lax.axis_size('peer')), 'peer', 0...]
    all_to_all x0 -> x1, starting transfers between devices: none -> 6.78 us  [per_device(): lax.all_to_all(jnp.stack([feat[None]] * lax.axis_size('peer')), 'peer', 0...]
    ppermute x4, starting transfers between devices: 15.2 us -> 12.5 us  [extended(): lax.ppermute(tail, axis, [(i, (i + 1) % count) for i in range(ends)])]
    another operation x0 -> x1, local copies, waits for them, and re-layouts: none -> 2.54 us  [per_device(): jnp.stack([feat[None]] * lax.axis_size('peer'))]
where the time goes in v1:
time: 139 us
  waiting for transfers between devices  76.8 us (55%)
  starting transfers between devices  28.1 us (20%)
  matrix products  26 us (19%)
  local copies, waits for them, and re-layouts  4.29 us (3%)
  other arithmetic  3.18 us (2%)
    all_to_all x1, waiting for transfers between devices, per_device(): lax.all_to_all(jnp.stack([feat[None]] * lax.axis_size('peer')), 'peer', 0...  57.2 us
    ppermute x4, waiting for transfers between devices, extended(): lax.ppermute(head, axis, [((i + 1) % count, i) for i in range(ends)])  19.7 us
    ppermute x4, starting transfers between devices, extended(): lax.ppermute(tail, axis, [(i, (i + 1) % count) for i in range(ends)])  12.5 us
    dot_general x18, matrix products, apply_dilated_filter(): jnp.einsum('rwi,io->rwo', input_window, filter_kernel[kernel_tap_row, ker...  10.6 us
    dot_general x18, matrix products, apply_dilated_filter(): jnp.einsum('rwo,io->rwi', input_window, filter_kernel[2 - kernel_tap_row,...  9.55 us
    ppermute x4, starting transfers between devices, extended(): lax.ppermute(head, axis, [((i + 1) % count, i) for i in range(ends)])  8.83 us
    all_to_all x1, starting transfers between devices, per_device(): lax.all_to_all(jnp.stack([feat[None]] * lax.axis_size('peer')), 'peer', 0...  6.78 us
    dot_general x1, matrix products, per_device(): jnp.einsum('k,krwc->rwc', pick, piece, preferred_element_type=jnp.float32)  5.9 us
  transfers between devices with their start and end apart: 9, of which 5 were waited for; matrix products, arithmetic and copies ran while one was open for 0% of the time, Pallas kernels for 0%

profile of v1, /device:TPU:97, one launch (start us, length us, event | category | flops | bytes accessed | tf_op | source)
XLA Modules:
  0.0 139.0 jit_solution(1108909621203328763)
XLA Ops:
  0.0 1.0 slice_bitcast_fusion.55
  1.0 5.4 %collective-permute-start = (bf16[2,32,512]{2,1,0:T(8,128)(2,1)S(1)}, bf16[2,32,512]{2,1,0:T(8,128)(2,1)S(1)}, u32[]{:S(2)}, u32[]{:S(2)}) collective-permute-start(bf16[2,32,512]{2,1,0:T(8,128)(2,1)S(1)} %get-tuple-element.11), channel_id=1, source_target_pairs={{0,1},{1,2},{2,3},{3,4},{4,5},{5,6},{6,7},{7,8},{8,9},{9,10},{10,1... | collective-permute-start | bytes 196616 | tf_op jit(solution)/shard_map/ppermute | solution.py:15
  6.5 1.9 %collective-permute-start.1 = (bf16[2,32,512]{2,1,0:T(8,128)(2,1)S(1)}, bf16[2,32,512]{2,1,0:T(8,128)(2,1)S(1)}, u32[]{:S(2)}, u32[]{:S(2)}) collective-permute-start(bf16[2,32,512]{2,1,0:T(8,128)(2,1)S(1)} %get-tuple-element.12), channel_id=1, source_target_pairs={{1,0},{2,1},{3,2},{4,3},{5,4},{6,5},{7,6},{8,7},{9,8},{10,9},{11,1... | collective-permute-start | bytes 196616 | tf_op jit(solution)/shard_map/ppermute | solution.py:17
  8.4 4.9 %collective-permute-done.1 = bf16[2,32,512]{2,1,0:T(8,128)(2,1)S(1)} collective-permute-done((bf16[2,32,512]{2,1,0:T(8,128)(2,1)S(1)}, bf16[2,32,512]{2,1,0:T(8,128)(2,1)S(1)}, u32[]{:S(2)}, u32[]{:S(2)}) %collective-permute-start.1) | collective-permute-done | bytes 65568 | tf_op jit(solution)/shard_map/ppermute | solution.py:17
  13.3 1.4 fusion.30
  14.7 1.5 %fusion.80 = f32[16,32,512]{2,1,0:T(8,128)S(1)} fusion(bf16[20,36,512]{2,1,0:T(8,128)(2,1)S(1)} %fusion.30, bf16[3,3,512,512]{3,2,1,0:T(8,128)(2,1)} %bitcast.164), kind=kOutput, calls=%fused_computation.131 | convolution fusion | flops 268435456 | bytes 2097152 | tf_op jit(solution)/shard_map/rwi,io->rwo/dot_general | solution.py:44
  16.1 1.6 %fusion.45 = f32[16,32,512]{2,1,0:T(8,128)S(1)} fusion(bf16[16,32,512]{2,1,0:T(8,128)(2,1)} %bitcast.185, bf16[2,32,512]{2,1,0:T(8,128)(2,1)S(1)} %collective-permute-done, bf16[3,3,512,512]{3,2,1,0:T(8,128)(2,1)} %bitcast.165), kind=kOutput, calls=%fused_computation.86 | convolution fusion | flops 269615104 | bytes 2162688 | tf_op jit(solution)/shard_map/rwi,io->rwo/dot_general | solution.py:44
  20.6 0.7 multiply_convert_fusion.1
  21.3 2.1 %collective-permute-start.2 = (bf16[4,32,512]{2,1,0:T(8,128)(2,1)S(1)}, bf16[4,32,512]{2,1,0:T(8,128)(2,1)S(1)}, u32[]{:S(2)}, u32[]{:S(2)}) collective-permute-start(bf16[4,32,512]{2,1,0:T(8,128)(2,1)S(1)} %get-tuple-element.9), channel_id=1, source_target_pairs={{0,1},{1,2},{2,3},{3,4},{4,5},{5,6},{6,7},{7,8},{8,9},{9,10},{10,1... | collective-permute-start | bytes 393224 | tf_op jit(solution)/shard_map/ppermute | solution.py:15
  23.3 2.4 %collective-permute-start.3 = (bf16[4,32,512]{2,1,0:T(8,128)(2,1)S(1)}, bf16[4,32,512]{2,1,0:T(8,128)(2,1)S(1)}, u32[]{:S(2)}, u32[]{:S(2)}) collective-permute-start(bf16[4,32,512]{2,1,0:T(8,128)(2,1)S(1)} %get-tuple-element.10), channel_id=1, source_target_pairs={{1,0},{2,1},{3,2},{4,3},{5,4},{6,5},{7,6},{8,7},{9,8},{10,9},{11,1... | collective-permute-start | bytes 393224 | tf_op jit(solution)/shard_map/ppermute | solution.py:17
  25.7 5.1 %collective-permute-done.3 = bf16[4,32,512]{2,1,0:T(8,128)(2,1)S(1)} collective-permute-done((bf16[4,32,512]{2,1,0:T(8,128)(2,1)S(1)}, bf16[4,32,512]{2,1,0:T(8,128)(2,1)S(1)}, u32[]{:S(2)}, u32[]{:S(2)}) %collective-permute-start.3) | collective-permute-done | bytes 131104 | tf_op jit(solution)/shard_map/ppermute | solution.py:17
  34.9 0.7 multiply_convert_fusion
  35.6 2.5 %stack.3 = bf16[8,1,16,32,512]{4,3,2,1,0:T(8,128)(2,1)} broadcast(bf16[16,32,512]{2,1,0:T(8,128)(2,1)S(1)} %get-tuple-element.15), dimensions={2,3,4} | broadcast | bytes 4718592 | tf_op jit(solution)/shard_map/stack | solution.py:89
  38.1 6.8 %all-to-all-start = ((bf16[8,1,16,32,512]{4,3,2,1,0:T(8,128)(2,1)}), bf16[8,1,16,32,512]{4,3,2,1,0:T(8,128)(2,1)}, u32[]{:S(2)}, u32[]{:S(2)}) async-start(bf16[8,1,16,32,512]{4,3,2,1,0:T(8,128)(2,1)} %stack.3), calls=%async_computation | async-start | bytes 8388608 | tf_op jit(solution)/shard_map/all_to_all | solution.py:89
  45.5 57.2 %all-to-all-done = bf16[8,1,16,32,512]{4,3,2,1,0:T(8,128)(2,1)} async-done(((bf16[8,1,16,32,512]{4,3,2,1,0:T(8,128)(2,1)}), bf16[8,1,16,32,512]{4,3,2,1,0:T(8,128)(2,1)}, u32[]{:S(2)}, u32[]{:S(2)}) %all-to-all-start) | async-done | bytes 4194336 | tf_op jit(solution)/shard_map/all_to_all | solution.py:89
  102.7 5.9 %fusion = f32[1,16,32,512]{3,0,2,1:T(1,128)S(1)} fusion(bf16[8,16,32,512]{3,2,1,0:T(8,128)(2,1)} %bitcast.49, s32[]{:T(128)} %bitcast.46), kind=kOutput, calls=%fused_computation | convolution fusion | flops 4194312 | bytes 5242884 | tf_op jit(solution)/shard_map/k,krwc->rwc/dot_general | solution.py:93
  109.2 2.9 %collective-permute-start.4 = (bf16[4,32,512]{2,1,0:T(8,128)(2,1)S(1)}, bf16[4,32,512]{2,1,0:T(8,128)(2,1)S(1)}, u32[]{:S(2)}, u32[]{:S(2)}) collective-permute-start(bf16[4,32,512]{2,1,0:T(8,128)(2,1)S(1)} %get-tuple-element.7), channel_id=1, source_target_pairs={{0,1},{1,2},{2,3},{3,4},{4,5},{5,6},{6,7},{7,8},{8,9},{9,10},{10,1... | collective-permute-start | bytes 393224 | tf_op jit(solution)/shard_map/ppermute | solution.py:15
  112.1 2.1 %collective-permute-start.5 = (bf16[4,32,512]{2,1,0:T(8,128)(2,1)S(1)}, bf16[4,32,512]{2,1,0:T(8,128)(2,1)S(1)}, u32[]{:S(2)}, u32[]{:S(2)}) collective-permute-start(bf16[4,32,512]{2,1,0:T(8,128)(2,1)S(1)} %get-tuple-element.8), channel_id=1, source_target_pairs={{1,0},{2,1},{3,2},{4,3},{5,4},{6,5},{7,6},{8,7},{9,8},{10,9},{11,1... | collective-permute-start | bytes 393224 | tf_op jit(solution)/shard_map/ppermute | solution.py:17
  114.2 5.4 %collective-permute-done.5 = bf16[4,32,512]{2,1,0:T(8,128)(2,1)S(1)} collective-permute-done((bf16[4,32,512]{2,1,0:T(8,128)(2,1)S(1)}, bf16[4,32,512]{2,1,0:T(8,128)(2,1)S(1)}, u32[]{:S(2)}, u32[]{:S(2)}) %collective-permute-start.5) | collective-permute-done | bytes 131104 | tf_op jit(solution)/shard_map/ppermute | solution.py:17
  123.9 0.7 fusion.15
  124.7 2.1 %collective-permute-start.6 = (bf16[2,32,512]{2,1,0:T(8,128)(2,1)S(1)}, bf16[2,32,512]{2,1,0:T(8,128)(2,1)S(1)}, u32[]{:S(2)}, u32[]{:S(2)}) collective-permute-start(bf16[2,32,512]{2,1,0:T(8,128)(2,1)S(1)} %get-tuple-element.5), channel_id=1, source_target_pairs={{0,1},{1,2},{2,3},{3,4},{4,5},{5,6},{6,7},{7,8},{8,9},{9,10},{10,1... | collective-permute-start | bytes 196616 | tf_op jit(solution)/shard_map/ppermute | solution.py:15
  126.7 2.4 %collective-permute-start.7 = (bf16[2,32,512]{2,1,0:T(8,128)(2,1)S(1)}, bf16[2,32,512]{2,1,0:T(8,128)(2,1)S(1)}, u32[]{:S(2)}, u32[]{:S(2)}) collective-permute-start(bf16[2,32,512]{2,1,0:T(8,128)(2,1)S(1)} %get-tuple-element.6), channel_id=1, source_target_pairs={{1,0},{2,1},{3,2},{4,3},{5,4},{6,5},{7,6},{8,7},{9,8},{10,9},{11,1... | collective-permute-start | bytes 196616 | tf_op jit(solution)/shard_map/ppermute | solution.py:17
  129.2 4.4 %collective-permute-done.7 = bf16[2,32,512]{2,1,0:T(8,128)(2,1)S(1)} collective-permute-done((bf16[2,32,512]{2,1,0:T(8,128)(2,1)S(1)}, bf16[2,32,512]{2,1,0:T(8,128)(2,1)S(1)}, u32[]{:S(2)}, u32[]{:S(2)}) %collective-permute-start.7) | collective-permute-done | bytes 65568 | tf_op jit(solution)/shard_map/ppermute | solution.py:17
  137.7 1.3 fusion.16
  (73 shorter events, 16.2 us)
Async XLA Ops:
  0.0 17.8 %copy-start = (bf16[1,3,3,512,512]{4,3,2,1,0:T(8,128)(2,1)S(1)}, bf16[1,3,3,512,512]{4,3,2,1,0:T(8,128)(2,1)}, u32[]{:S(2)}) copy-start(bf16[1,3,3,512,512]{4,3,2,1,0:T(8,128)(2,1)} %param.12) | copy-start | bytes 14155780
  1.0 7.4 %collective-permute-start = (bf16[2,32,512]{2,1,0:T(8,128)(2,1)S(1)}, bf16[2,32,512]{2,1,0:T(8,128)(2,1)S(1)}, u32[]{:S(2)}, u32[]{:S(2)}) collective-permute-start(bf16[2,32,512]{2,1,0:T(8,128)(2,1)S(1)} %get-tuple-element.11), channel_id=1, source_target_pairs={{0,1},{1,2},{2,3},{3,4},{4,5},{5,6},{6,7},{7,8},{8,9},{9,10},{10,1... | collective-permute-start | bytes 196616 | tf_op jit(solution)/shard_map/ppermute | solution.py:15
  6.5 6.8 %collective-permute-start.1 = (bf16[2,32,512]{2,1,0:T(8,128)(2,1)S(1)}, bf16[2,32,512]{2,1,0:T(8,128)(2,1)S(1)}, u32[]{:S(2)}, u32[]{:S(2)}) collective-permute-start(bf16[2,32,512]{2,1,0:T(8,128)(2,1)S(1)} %get-tuple-element.12), channel_id=1, source_target_pairs={{1,0},{2,1},{3,2},{4,3},{5,4},{6,5},{7,6},{8,7},{9,8},{10,9},{11,1... | collective-permute-start | bytes 196616 | tf_op jit(solution)/shard_map/ppermute | solution.py:17
  17.8 1.4 copy-start.1
  19.1 1.4 %copy-start.4 = (f32[1,512]{1,0:T(1,128)S(1)}, f32[1,512]{1,0:T(1,128)}, u32[]{:S(2)}) copy-start(f32[1,512]{1,0:T(1,128)} %param.14) | copy-start | bytes 6148
  19.2 1.4 copy-start.6
  20.1 11.2 %slice-start = ((s8[4718592]{0:T(1024)(128)(4,1)}), s8[4194304]{0:T(1024)(128)(4,1)S(1)}, s32[]{:S(2)}) async-start(s8[4718592]{0:T(1024)(128)(4,1)} %bitcast.142), calls=%async_computation.1 | async-start | bytes 8388608
  20.5 10.7 %slice-start.1 = ((s8[4718592]{0:T(1024)(128)(4,1)}), s8[524288]{0:T(1024)(128)(4,1)S(1)}, s32[]{:S(2)}) async-start(s8[4718592]{0:T(1024)(128)(4,1)} %bitcast.142), calls=%async_computation.2 | async-start | bytes 1048576
  21.3 4.5 %collective-permute-start.2 = (bf16[4,32,512]{2,1,0:T(8,128)(2,1)S(1)}, bf16[4,32,512]{2,1,0:T(8,128)(2,1)S(1)}, u32[]{:S(2)}, u32[]{:S(2)}) collective-permute-start(bf16[4,32,512]{2,1,0:T(8,128)(2,1)S(1)} %get-tuple-element.9), channel_id=1, source_target_pairs={{0,1},{1,2},{2,3},{3,4},{4,5},{5,6},{6,7},{7,8},{8,9},{9,10},{10,1... | collective-permute-start | bytes 393224 | tf_op jit(solution)/shard_map/ppermute | solution.py:15
  23.3 7.5 %collective-permute-start.3 = (bf16[4,32,512]{2,1,0:T(8,128)(2,1)S(1)}, bf16[4,32,512]{2,1,0:T(8,128)(2,1)S(1)}, u32[]{:S(2)}, u32[]{:S(2)}) collective-permute-start(bf16[4,32,512]{2,1,0:T(8,128)(2,1)S(1)} %get-tuple-element.10), channel_id=1, source_target_pairs={{1,0},{2,1},{3,2},{4,3},{5,4},{6,5},{7,6},{8,7},{9,8},{10,9},{11,1... | collective-permute-start | bytes 393224 | tf_op jit(solution)/shard_map/ppermute | solution.py:17
  33.5 1.4 copy-start.3
  33.5 1.4 copy-start.5
  38.1 6.8 %copy-start.7 = (s32[8]{0:T(128)S(1)}, s32[8]{0:T(128)}, u32[]{:S(2)}) copy-start(s32[8]{0:T(128)} %param.11) | copy-start | bytes 100
  38.1 82.0 %slice-start.2 = ((s8[4718592]{0:T(1024)(128)(4,1)}), s8[524288]{0:T(1024)(128)(4,1)S(1)}, s32[]{:S(2)}) async-start(s8[4718592]{0:T(1024)(128)(4,1)} %bitcast.153), calls=%async_computation.3 | async-start | bytes 1048576
  38.1 64.5 %all-to-all-start = ((bf16[8,1,16,32,512]{4,3,2,1,0:T(8,128)(2,1)}), bf16[8,1,16,32,512]{4,3,2,1,0:T(8,128)(2,1)}, u32[]{:S(2)}, u32[]{:S(2)}) async-start(bf16[8,1,16,32,512]{4,3,2,1,0:T(8,128)(2,1)} %stack.3), calls=%async_computation | async-start | bytes 8388608 | tf_op jit(solution)/shard_map/all_to_all | solution.py:89
  44.9 63.7 %copy-start.2 = (bf16[1,16,32,512]{3,2,1,0:T(8,128)(2,1)S(1)}, bf16[1,16,32,512]{3,2,1,0:T(8,128)(2,1)}, u32[]{:S(2)}) copy-start(bf16[1,16,32,512]{3,2,1,0:T(8,128)(2,1)} %param.10) | copy-start | bytes 1572868
  102.6 17.4 %slice-start.3 = ((s8[4718592]{0:T(1024)(128)(4,1)}), s8[4194304]{0:T(1024)(128)(4,1)S(1)}, s32[]{:S(2)}) async-start(s8[4718592]{0:T(1024)(128)(4,1)} %bitcast.153), calls=%async_computation.4 | async-start | bytes 8388608
  109.2 5.0 %collective-permute-start.4 = (bf16[4,32,512]{2,1,0:T(8,128)(2,1)S(1)}, bf16[4,32,512]{2,1,0:T(8,128)(2,1)S(1)}, u32[]{:S(2)}, u32[]{:S(2)}) collective-permute-start(bf16[4,32,512]{2,1,0:T(8,128)(2,1)S(1)} %get-tuple-element.7), channel_id=1, source_target_pairs={{0,1},{1,2},{2,3},{3,4},{4,5},{5,6},{6,7},{7,8},{8,9},{9,10},{10,1... | collective-permute-start | bytes 393224 | tf_op jit(solution)/shard_map/ppermute | solution.py:15
  112.1 7.5 %collective-permute-start.5 = (bf16[4,32,512]{2,1,0:T(8,128)(2,1)S(1)}, bf16[4,32,512]{2,1,0:T(8,128)(2,1)S(1)}, u32[]{:S(2)}, u32[]{:S(2)}) collective-permute-start(bf16[4,32,512]{2,1,0:T(8,128)(2,1)S(1)} %get-tuple-element.8), channel_id=1, source_target_pairs={{1,0},{2,1},{3,2},{4,3},{5,4},{6,5},{7,6},{8,7},{9,8},{10,9},{11,1... | collective-permute-start | bytes 393224 | tf_op jit(solution)/shard_map/ppermute | solution.py:17
  123.4 10.5 %slice-start.4 = ((s8[4718592]{0:T(1024)(128)(4,1)}), s8[4194304]{0:T(1024)(128)(4,1)S(1)}, s32[]{:S(2)}) async-start(s8[4718592]{0:T(1024)(128)(4,1)} %bitcast.173), calls=%async_computation.5 | async-start | bytes 8388608
  123.9 10.0 %slice-start.5 = ((s8[4718592]{0:T(1024)(128)(4,1)}), s8[524288]{0:T(1024)(128)(4,1)S(1)}, s32[]{:S(2)}) async-start(s8[4718592]{0:T(1024)(128)(4,1)} %bitcast.173), calls=%async_computation.6 | async-start | bytes 1048576
  124.7 4.5 %collective-permute-start.6 = (bf16[2,32,512]{2,1,0:T(8,128)(2,1)S(1)}, bf16[2,32,512]{2,1,0:T(8,128)(2,1)S(1)}, u32[]{:S(2)}, u32[]{:S(2)}) collective-permute-start(bf16[2,32,512]{2,1,0:T(8,128)(2,1)S(1)} %get-tuple-element.5), channel_id=1, source_target_pairs={{0,1},{1,2},{2,3},{3,4},{4,5},{5,6},{6,7},{7,8},{8,9},{9,10},{10,1... | collective-permute-start | bytes 196616 | tf_op jit(solution)/shard_map/ppermute | solution.py:15
  126.7 6.8 %collective-permute-start.7 = (bf16[2,32,512]{2,1,0:T(8,128)(2,1)S(1)}, bf16[2,32,512]{2,1,0:T(8,128)(2,1)S(1)}, u32[]{:S(2)}, u32[]{:S(2)}) collective-permute-start(bf16[2,32,512]{2,1,0:T(8,128)(2,1)S(1)} %get-tuple-element.6), channel_id=1, source_target_pairs={{1,0},{2,1},{3,2},{4,3},{5,4},{6,5},{7,6},{8,7},{9,8},{10,9},{11,1... | collective-permute-start | bytes 196616 | tf_op jit(solution)/shard_map/ppermute | solution.py:17
